TPU v7x, 128 devices: a whole 4x4x4 slice. The times are simulated.
128 devices in a mesh: ping: 16 (over x, z), band: 8 (over y, core).
Axes of the slice: x: 4, y: 4, z: 4, core: 2. Of those that a mesh axis runs over, the one named last changes fastest.
Arguments:
- echoes: bfloat16 [2048, 8, 2, 8192], P(('ping', 'band')), may hold values from -6 to 6
- replica: bfloat16 [8, 2, 128], replicated, may hold values from -0.375 to 0.375
- steering: bfloat16 [2, 64, 64], replicated, may hold values from -0.5 to 0.5
- angle_weights: bfloat16 [2, 128, 64], replicated, may hold values from -0.75 to 0.75
- range_weights: bfloat16 [64, 384, 128], P('band'), may hold values from -0.3125 to 0.3125
- range_offsets: int32 [64], P('band'), may hold values from 0 to 5
- merge_owner: int32 [256], replicated, may hold values from -1 to 15, as said below
- merge_slot: int32 [256], replicated, may hold values from 0 to 7
Outputs:
- merged: bfloat16 [128, 2, 128, 8192], P('ping', None, None, 'band')
Inputs may be any that keep to these rules, and one draw needn't show every extreme that they name: `merge_owner`: -1 marks a block that is not kept. Among the 16 blocks of one ping index (aligned blocks of the list) at most 2 name the same owner, and in every draw one owner is named by exactly 2 blocks of every ping index.
All inputs are finite; a program needn't handle non-finite values.
Results may differ from a plain program's by a relative error of at most 0.007.
Values may be sent and summed in bfloat16 or wider, within the bound.
No kernel may reach another device: no remote copies, remote signals or barrier semaphores. Data moves between devices by JAX's collectives and lax.ppermute only.
A program may use at most 128 MiB of HBM per device.

v0:
```python
import jax
import jax.numpy as jnp
from jax import lax
from jax.sharding import PartitionSpec as P

SUB_PINGS = 8


def toeplitz_blocks(replica):
    taps_count = replica.shape[2]
    shifts = jnp.arange(taps_count)
    row_index = jnp.arange(taps_count)[:, None]
    col_index = jnp.arange(taps_count)[None, :]
    lower_sel = ((row_index - col_index)[None] == shifts[:, None, None]).astype(jnp.float32)
    upper_sel = ((row_index - col_index + taps_count)[None] == shifts[:, None, None]).astype(
        jnp.float32
    )
    real_taps = replica[:, 0].astype(jnp.float32)
    imag_taps = replica[:, 1].astype(jnp.float32)
    high = lax.Precision.HIGHEST
    lower_real = jnp.einsum("ck,kmn->cmn", real_taps, lower_sel, precision=high)
    lower_imag = jnp.einsum("ck,kmn->cmn", imag_taps, lower_sel, precision=high)
    upper_real = jnp.einsum("ck,kmn->cmn", real_taps, upper_sel, precision=high)
    upper_imag = jnp.einsum("ck,kmn->cmn", imag_taps, upper_sel, precision=high)
    layers = [
        jnp.concatenate([lower_real, -lower_imag], 2),
        jnp.concatenate([lower_imag, lower_real], 2),
        jnp.concatenate([upper_real, -upper_imag], 2),
        jnp.concatenate([upper_imag, upper_real], 2),
    ]
    return jnp.concatenate(layers, 1).astype(jnp.bfloat16)


def compress(echo_part, toeplitz):
    pings, chans, parts, bins = echo_part.shape
    taps_count = toeplitz.shape[2] // 2
    block_count = bins // taps_count
    shaped = echo_part.reshape(pings, chans, parts, block_count, taps_count)
    weights = toeplitz.reshape(chans, 2, parts, taps_count, 2, taps_count)
    lower = jnp.einsum(
        "pcqbk,cqkon->pcobn", shaped, weights[:, 0], preferred_element_type=jnp.float32
    )
    upper = jnp.einsum(
        "pcqbk,cqkon->pcobn", shaped, weights[:, 1], preferred_element_type=jnp.float32
    )
    moved = jnp.concatenate([upper[:, :, :, 1:], jnp.zeros_like(upper[:, :, :, :1])], axis=3)
    total = lower + moved
    return total.reshape(pings, chans, 2, bins).astype(jnp.bfloat16)


def beamform(tile, steering, sub_pings):
    pings, chans, parts, bins = tile.shape
    blocks = pings // sub_pings
    grouped = tile.reshape(blocks, sub_pings * chans * parts, bins)
    real_steer = steering[0]
    imag_steer = steering[1]
    beam_count = real_steer.shape[0]
    mixer = jnp.concatenate(
        [
            jnp.concatenate([real_steer, -imag_steer], 1),
            jnp.concatenate([imag_steer, real_steer], 1),
        ],
        0,
    )
    mixer = (
        mixer.reshape(2 * beam_count, 2, sub_pings * chans)
        .transpose(0, 2, 1)
        .reshape(2 * beam_count, -1)
    )
    beams = jnp.einsum("yx,bxr->byr", mixer, grouped, preferred_element_type=jnp.float32)
    return beams.reshape(blocks, 2, beam_count, bins).astype(jnp.bfloat16)


def rotate_angles(beam_image, angle_weights, parity):
    matrices = jnp.where(parity[:, None, None] == 1, angle_weights[1], angle_weights[0])
    turned = jnp.einsum("bya,bpar->bpyr", matrices, beam_image, preferred_element_type=jnp.float32)
    return turned.astype(jnp.bfloat16)


def dense_interp(range_weights, range_offsets):
    count = range_weights.shape[0]
    selector = (
        jnp.arange(count)[None, None, :]
        == (range_offsets[:, None] + jnp.arange(3)[None, :])[:, :, None]
    ).astype(jnp.bfloat16)
    pieces = range_weights.reshape(count, 3, 128, 128)
    dense = jnp.einsum("jtb,jtin->bijn", selector, pieces, preferred_element_type=jnp.float32)
    return dense.astype(jnp.bfloat16).reshape(count * 128, count * 128)


def range_interp(turned, dense):
    flat = turned.reshape(-1, turned.shape[3])
    product = jnp.dot(flat, dense, preferred_element_type=jnp.float32)
    return product.astype(jnp.bfloat16).reshape(turned.shape)


def pack_rows(packer, source):
    flat = jnp.dot(packer, source.reshape(source.shape[0], -1), preferred_element_type=jnp.float32)
    return flat.astype(jnp.bfloat16).reshape((packer.shape[0],) + source.shape[1:])


def on_device(
    echoes, replica, steering, angle_weights, range_weights, range_offsets, merge_owner, merge_slot
):
    ping_count = lax.axis_size("ping")
    ping_index = lax.axis_index("ping")
    toeplitz = toeplitz_blocks(replica)
    compressed = compress(echoes, toeplitz)
    band_tile = lax.all_to_all(compressed, "band", split_axis=3, concat_axis=0, tiled=True)
    beam_image = beamform(band_tile, steering, SUB_PINGS)
    blocks_here = beam_image.shape[0]
    capacity = max(2, (blocks_here + ping_count - 1) // ping_count)
    slot_count = blocks_here // 2
    routes = merge_owner.reshape(ping_count, blocks_here)
    slots_all = merge_slot.reshape(ping_count, blocks_here)
    my_routes = lax.dynamic_index_in_dim(routes, ping_index, 0, keepdims=False)
    target_hot = (my_routes[:, None] == jnp.arange(ping_count)[None, :]).astype(jnp.int32)
    rank_send = jnp.sum(jnp.cumsum(target_hot, 0) * target_hot, 1) - 1
    packer = (target_hot.T[:, None, :] == 1) & (
        rank_send[None, None, :] == jnp.arange(capacity)[None, :, None]
    )
    packer = packer.reshape(ping_count * capacity, blocks_here).astype(jnp.bfloat16)
    owned = (routes == ping_index).astype(jnp.int32)
    rank_recv = jnp.cumsum(owned, 1) * owned - 1
    matched = (owned[:, None, :] == 1) & (
        rank_recv[:, None, :] == jnp.arange(capacity)[None, :, None]
    )
    matched_float = matched.astype(jnp.float32)
    slot_hot = (slots_all[:, :, None] == jnp.arange(slot_count)[None, None, :]).astype(jnp.float32)
    combiner = jnp.einsum("scb,sbo->osc", matched_float, slot_hot).reshape(
        slot_count, ping_count * capacity
    )
    combiner = combiner.astype(jnp.bfloat16)
    dense = dense_interp(range_weights, range_offsets)
    my_parity = (ping_index * blocks_here + jnp.arange(blocks_here)) % 2
    images = range_interp(rotate_angles(beam_image, angle_weights, my_parity), dense)
    outgoing = pack_rows(packer, images)
    arrived = lax.all_to_all(outgoing, "ping", split_axis=0, concat_axis=0, tiled=True)
    merged = jnp.dot(
        combiner, arrived.reshape(arrived.shape[0], -1), preferred_element_type=jnp.float32
    )
    return merged.reshape((slot_count,) + arrived.shape[1:]).astype(jnp.bfloat16)


def solution(mesh):
    placed = (
        P(("ping", "band"), None, None, None),
        P(),
        P(),
        P(),
        P("band", None, None),
        P("band"),
        P(),
        P(),
    )
    return jax.shard_map(
        on_device,
        mesh=mesh,
        in_specs=placed,
        out_specs=P("ping", None, None, "band"),
        check_vma=False,
    )
```

profile of v0, /device:TPU:68, one launch (start us, length us, event | category | flops | bytes accessed | tf_op | source)
XLA Modules:
  0.0 673.8 jit_solution(3247890180094275025)
XLA Ops:
  0.0 0.0 copy-start
  0.0 0.8 fusion.50
  0.8 1.3 fusion.3
  2.2 1.3 fusion.27
  3.5 1.3 fusion.28
  4.8 1.4 fusion.30
  6.3 9.8 %maximum_maximum_fusion = bf16[8,512,256]{2,0,1:T(8,128)(2,1)S(1)} fusion(bf16[8,128,128]{2,0,1:T(8,128)(2,1)S(1)} %fusion.27, bf16[8,128,128]{2,0,1:T(8,128)(2,1)S(1)} %get-tuple-element.21, bf16[8,128,128]{2,0,1:T(8,128)(2,1)S(1)} %get-tuple-element.22, bf16[8,128,128]{2,0,1:T(8,128)(2,1)S(1)} %fusion.28, bf16[8,128,128]{2,0,1:T(8,128)(2,1)S(1)} %get-tuple-element.10, ...), kind=kLoop, calls=%fused_computation.26 | loop fusion | flops 16777216 | bytes 3670016 | tf_op jit(solution)/shard_map/concatenate | solution.py:31
  16.1 0.4 fusion.48
  16.5 7.8 %reshape.188 = bf16[16,8,2,64,128]{4,3,2,1,0:T(8,128)(2,1)} reshape(bf16[16,8,2,8192]{3,2,1,0:T(2,128)(2,1)} %param.8) | data formatting | bytes 8388608 | tf_op jit(solution)/shard_map/reshape | solution.py:38
  24.3 6.7 fusion.15
  31.0 0.0 copy-start.2
  31.0 4.7 slice.38
  35.6 0.0 copy-done.2
  35.6 2.9 fusion.2
  38.6 48.6 %copy.68 = bf16[16,8,2,64,128]{0,2,1,4,3:T(2,128)(2,1)} copy(bf16[16,8,2,64,128]{4,3,0,2,1:T(8,128)(2,1)} %fusion.2) | data formatting | bytes 8388608 | tf_op jit(solution)/shard_map/convert_element_type | solution.py:48
  87.2 37.8 %reshape.209 = bf16[8,2,131072]{2,1,0:T(2,128)(2,1)} reshape(bf16[8192,8,2,16]{3,2,1,0:T(2,128)(2,1)} %bitcast.128) | data formatting | bytes 8388608
  125.1 0.0 copy-start.3
  125.1 0.0 copy-start.7
  125.1 4.7 all-to-all-start
  129.8 0.0 copy-start.5
  129.8 0.0 copy-start.4
  129.8 0.0 copy-done.3
  129.8 0.1 copy.75
  129.9 0.1 copy.74
  130.0 0.1 maximum_maximum_fusion.1
  130.2 0.0 copy-done.7
  130.2 0.1 iota_add_fusion
  130.2 0.0 copy-done
  130.3 1.2 convert_bitcast_fusion
  131.5 2.7 copy.49
  134.2 0.0 copy-done.5
  134.2 0.1 reshape.187
  134.2 0.1 convert_compare_fusion
  134.4 0.2 select_reduce_fusion
  134.6 0.0 copy-done.4
  134.7 44.8 %all-to-all-done = bf16[8,2,131072]{2,1,0:T(2,128)(2,1)} async-done(((bf16[8,2,131072]{2,1,0:T(2,128)(2,1)}), bf16[8,2,131072]{2,1,0:T(2,128)(2,1)}, u32[]{:S(2)}, u32[]{:S(2)}) %all-to-all-start) | async-done | bytes 4194336 | tf_op jit(solution)/shard_map/all_to_all | solution.py:109
  179.4 25.7 %reshape.210 = bf16[8192,8,2,16]{3,2,1,0:T(2,128)(2,1)} reshape(bf16[8,2,131072]{2,1,0:T(2,128)(2,1)} %all-to-all-done) | data formatting | bytes 8388608
  205.2 76.8 %copy.43 = bf16[16,8,2,8,1024]{4,2,1,0,3:T(2,128)(2,1)} copy(bf16[16,8,2,8,1024]{0,2,1,4,3:T(2,128)(2,1)} %bitcast.129) | data formatting | bytes 8388608 | tf_op jit(solution)/shard_map/all_to_all | solution.py:109
  282.0 7.2 %reshape.189 = bf16[16,128,1024]{2,1,0:T(8,128)(2,1)} reshape(bf16[8,16,8,2,1024]{4,3,2,1,0:T(2,128)(2,1)} %bitcast.132) | data formatting | bytes 8388608 | tf_op jit(solution)/shard_map/reshape | solution.py:54
  289.2 3.7 convolution_convert_fusion.3
  292.9 2.4 convolution_convert_fusion.2
  295.4 12.4 %convolution_convert_fusion.1 = bf16[4096,1024]{1,0:T(8,128)(2,1)} fusion(bf16[4096,1024]{1,0:T(8,128)(2,1)S(1)} %bitcast.134, bf16[128,8,8,128]{3,2,1,0:T(8,128)(2,1)} %bitcast.136), kind=kOutput, calls=%fused_computation.11 | convolution fusion | flops 8594128896 | bytes 18874368 | tf_op jit(solution)/shard_map/dot_general | solution.py:93
  307.8 8.1 %reshape_reshape.3 = bf16[16,262144]{1,0:T(8,128)(2,1)} reshape(bf16[4096,1024]{1,0:T(8,128)(2,1)} %convolution_convert_fusion.1) | data formatting | bytes 16777216 | tf_op jit(solution)/shard_map/reshape;reshape | solution.py:98
  316.0 13.6 %convolution_convert_fusion = bf16[32,262144]{1,0:T(8,128)(2,1)} fusion(pred[32,16]{1,0:T(32,128)(4,1)S(1)} %and.49, bf16[16,262144]{1,0:T(8,128)(2,1)} %reshape_reshape.3), kind=kOutput, calls=%fused_computation | convolution fusion | flops 276824064 | bytes 25166336 | tf_op jit(solution)/shard_map/dot_general | solution.py:98
  329.5 18.7 %copy.77 = bf16[4,8,256,1024]{3,2,1,0:T(8,128)(2,1)} copy(bf16[4,8,256,1024]{3,1,2,0:T(8,128)(2,1)} %bitcast.131) | data formatting | bytes 33554432
  348.3 0.0 copy-start.6
  348.3 7.9 %all-to-all-start.1 = ((bf16[32,2,128,1024]{3,2,1,0:T(8,128)(2,1)}), bf16[32,2,128,1024]{3,2,1,0:T(8,128)(2,1)}, u32[]{:S(2)}, u32[]{:S(2)}) async-start(bf16[32,2,128,1024]{3,2,1,0:T(8,128)(2,1)} %bitcast.130), calls=%async_computation.1 | async-start | bytes 33554432 | tf_op jit(solution)/shard_map/all_to_all | solution.py:138
  356.2 0.2 reduce_window_sum.22
  356.4 0.0 copy-done.6
  356.4 0.1 eq.166
  356.5 0.1 convolution_convert_fusion.4
  356.6 295.7 %all-to-all-done.1 = bf16[32,2,128,1024]{3,2,1,0:T(8,128)(2,1)} async-done(((bf16[32,2,128,1024]{3,2,1,0:T(8,128)(2,1)}), bf16[32,2,128,1024]{3,2,1,0:T(8,128)(2,1)}, u32[]{:S(2)}, u32[]{:S(2)}) %all-to-all-start.1) | async-done | bytes 16777248 | tf_op jit(solution)/shard_map/all_to_all | solution.py:138
  652.3 0.0 copy-start.1
  652.3 16.6 %fusion.20 = bf16[8,2,128,1024]{3,0,2,1:T(8,128)(2,1)S(1)} fusion(bf16[8,32,1,1]{0,1,3,2:T(8,128)(2,1)S(1)} %bitcast.141, bf16[2,128,1024,32]{2,1,0,3:T(8,128)(2,1)} %bitcast.76), kind=kOutput, calls=%fused_computation.22 | convolution fusion | flops 136314880 | bytes 20972032 | tf_op jit(solution)/shard_map/dot_general | solution.py:139
  669.0 4.4 copy.52
  673.3 0.0 copy-done.1
  (16 shorter events, 0.2 us)
Async XLA Ops:
  0.0 130.3 %copy-start = (bf16[8,384,128]{2,1,0:T(8,128)(2,1)S(1)}, bf16[8,384,128]{2,1,0:T(8,128)(2,1)}, u32[]{:S(2)}) copy-start(bf16[8,384,128]{2,1,0:T(8,128)(2,1)} %param.12) | copy-start | bytes 2359300
  31.0 4.7 copy-start.2
  125.1 4.7 copy-start.3
  125.1 5.1 copy-start.7
  125.1 54.4 %all-to-all-start = ((bf16[8,2,131072]{2,1,0:T(2,128)(2,1)}), bf16[8,2,131072]{2,1,0:T(2,128)(2,1)}, u32[]{:S(2)}, u32[]{:S(2)}) async-start(bf16[8,2,131072]{2,1,0:T(2,128)(2,1)} %reshape.209), calls=%async_computation | async-start | bytes 8388608 | tf_op jit(solution)/shard_map/all_to_all | solution.py:109
  129.8 4.4 copy-start.5
  129.8 4.8 copy-start.4
  348.3 8.1 %copy-start.6 = (s32[256]{0:T(256)S(1)}, s32[256]{0:T(256)}, u32[]{:S(2)}) copy-start(s32[256]{0:T(256)} %param.15) | copy-start | bytes 3076
  348.3 304.1 %all-to-all-start.1 = ((bf16[32,2,128,1024]{3,2,1,0:T(8,128)(2,1)}), bf16[32,2,128,1024]{3,2,1,0:T(8,128)(2,1)}, u32[]{:S(2)}, u32[]{:S(2)}) async-start(bf16[32,2,128,1024]{3,2,1,0:T(8,128)(2,1)} %bitcast.130), calls=%async_computation.1 | async-start | bytes 33554432 | tf_op jit(solution)/shard_map/all_to_all | solution.py:138
  652.3 21.0 %copy-start.1 = (bf16[8,384,128]{2,1,0:T(8,128)(2,1)S(1)}, bf16[8,384,128]{2,1,0:T(8,128)(2,1)}, u32[]{:S(2)}) copy-start(bf16[8,384,128]{2,1,0:T(8,128)(2,1)} %param.12) | copy-start | bytes 2359300
where the time goes:
time: 684 us; the launch traced here: 674 us
  waiting for transfers between devices  340 us (50%)
  local copies, waits for them, and re-layouts  244 us (36%)
  matrix products  65.2 us (10%)
  starting transfers between devices  12.6 us (2%)
  other arithmetic  10.5 us (2%)
    all_to_all x1, waiting for transfers between devices, on_device(): lax.all_to_all(outgoing, 'ping', split_axis=0, concat_axis=0, tiled=True)  296 us
    unnamed x21, local copies, waits for them, and re-layouts  82.5 us
    all_to_all x1, local copies, waits for them, and re-layouts, on_device(): lax.all_to_all(compressed, 'band', split_axis=3, concat_axis=0, tiled=True)  76.8 us
    convert_element_type x1, local copies, waits for them, and re-layouts, compress(): return total.reshape(pings, chans, 2, bins).astype(jnp.bfloat16)  48.6 us
    all_to_all x1, waiting for transfers between devices, on_device(): lax.all_to_all(compressed, 'band', split_axis=3, concat_axis=0, tiled=True)  44.8 us
    dot_general x1, matrix products, on_device(): jnp.dot(combiner, arrived.reshape(arrived.shape[0], -1), preferred_elemen...  16.6 us
  transfers between devices with their start and end apart: 2, of which 2 were waited for; matrix products, arithmetic and copies ran while one was open for 1% of the time, Pallas kernels for 0%

commit v1 on v0

--- a/solution.py
+++ b/solution.py
@@ -106,7 +106,19 @@
     ping_index = lax.axis_index("ping")
     toeplitz = toeplitz_blocks(replica)
     compressed = compress(echoes, toeplitz)
-    band_tile = lax.all_to_all(compressed, "band", split_axis=3, concat_axis=0, tiled=True)
+    ways, here = (lax.axis_size("band"), lax.axis_index("band"))
+    width = compressed.shape[3] // ways
+    shape = list(compressed.shape)
+    shape[3] = width
+    height = shape[0]
+    shape[0] = height * ways
+    full = jnp.zeros(shape, compressed.dtype)
+    for mask in range(ways):
+        part = lax.dynamic_slice_in_dim(compressed, (here ^ mask) * width, width, axis=3)
+        if mask:
+            part = lax.ppermute(part, "band", [(d, d ^ mask) for d in range(ways)])
+        full = lax.dynamic_update_slice_in_dim(full, part, (here ^ mask) * height, axis=0)
+    band_tile = full
     beam_image = beamform(band_tile, steering, SUB_PINGS)
     blocks_here = beam_image.shape[0]
     capacity = max(2, (blocks_here + ping_count - 1) // ping_count)

time: 684 us -> 511 us (0.75)
  local copies, waits for them, and re-layouts: 244 us -> 89 us
  waiting for transfers between devices: 340 us -> 323 us
    all_to_all x1 -> x0, local copies, waits for them, and re-layouts: 76.8 us -> none  [on_device(): lax.all_to_all(compressed, 'band', split_axis=3, concat_axis=0, tiled=True)]
    unnamed x21, local copies, waits for them, and re-layouts: 82.5 us -> 18.9 us
    all_to_all x1 -> x0, waiting for transfers between devices: 44.8 us -> none  [on_device(): lax.all_to_all(compressed, 'band', split_axis=3, concat_axis=0, tiled=True)]
    convert_element_type x1, local copies, waits for them, and re-layouts: 48.6 us -> 7.3 us  [compress(): return total.reshape(pings, chans, 2, bins).astype(jnp.bfloat16)]
    ppermute x0 -> x7, waiting for transfers between devices: none -> 22.7 us  [on_device(): part = lax.ppermute(part, 'band', [(d, d ^ mask) for d in range(ways)])]
    dynamic_update_slice x0 -> x8, local copies, waits for them, and re-layouts: none -> 15.9 us  [on_device(): lax.dynamic_update_slice_in_dim(full, part, (here ^ mask) * height, axis=0)]
    ppermute x0 -> x7, starting transfers between devices: none -> 8.84 us  [on_device(): part = lax.ppermute(part, 'band', [(d, d ^ mask) for d in range(ways)])]
  transfers between devices with their start and end apart: 2 -> 8, of which waited for: 2 -> 4; matrix products, arithmetic and copies ran while one was open for 1% -> 5% of each run, Pallas kernels for 0% -> 0%
where the time goes in v1:
time: 511 us; the launch traced here: 505 us
  waiting for transfers between devices  323 us (63%)
  local copies, waits for them, and re-layouts  89 us (17%)
  matrix products  65.5 us (13%)
  starting transfers between devices  16.7 us (3%)
  other arithmetic  10.5 us (2%)
    all_to_all x1, waiting for transfers between devices, on_device(): lax.all_to_all(outgoing, 'ping', split_axis=0, concat_axis=0, tiled=True)  300 us
    ppermute x7, waiting for transfers between devices, on_device(): part = lax.ppermute(part, 'band', [(d, d ^ mask) for d in range(ways)])  22.7 us
    unnamed x21, local copies, waits for them, and re-layouts  18.9 us
    dot_general x1, matrix products, on_device(): jnp.dot(combiner, arrived.reshape(arrived.shape[0], -1), preferred_elemen...  16.6 us
    dynamic_update_slice x8, local copies, waits for them, and re-layouts, on_device(): lax.dynamic_update_slice_in_dim(full, part, (here ^ mask) * height, axis=0)  15.9 us
    dot_general x1, matrix products, pack_rows(): jnp.dot(packer, source.reshape(source.shape[0], -1), preferred_element_ty...  13.6 us
    dot_general x1, matrix products, range_interp(): product = jnp.dot(flat, dense, preferred_element_type=jnp.float32)  12.4 us
  transfers between devices with their start and end apart: 8, of which 4 were waited for; matrix products, arithmetic and copies ran while one was open for 5% of the time, Pallas kernels for 0%

profile of v1, /device:TPU:68, one launch (start us, length us, event | category | flops | bytes accessed | tf_op | source)
XLA Modules:
  0.0 505.4 jit_solution(11004634623604229468)
XLA Ops:
  0.0 0.0 copy-start
  0.0 0.8 fusion.51
  0.8 1.3 fusion.28
  2.2 1.3 fusion.27
  3.5 1.3 fusion.3
  4.8 1.4 fusion.30
  6.3 9.8 %maximum_maximum_fusion = bf16[8,512,256]{2,0,1:T(8,128)(2,1)S(1)} fusion(bf16[8,128,128]{2,0,1:T(8,128)(2,1)S(1)} %fusion.27, bf16[8,128,128]{2,0,1:T(8,128)(2,1)S(1)} %get-tuple-element.31, bf16[8,128,128]{2,0,1:T(8,128)(2,1)S(1)} %get-tuple-element.32, bf16[8,128,128]{2,0,1:T(8,128)(2,1)S(1)} %fusion.28, bf16[8,128,128]{2,0,1:T(8,128)(2,1)S(1)} %get-tuple-element.18, ...), kind=kLoop, calls=%fused_computation.26 | loop fusion | flops 16777216 | bytes 3670016 | tf_op jit(solution)/shard_map/concatenate | solution.py:31
  16.1 0.4 fusion.49
  16.5 7.8 %reshape.187 = bf16[16,8,2,64,128]{4,3,2,1,0:T(8,128)(2,1)} reshape(bf16[16,8,2,8192]{3,2,1,0:T(2,128)(2,1)} %param.8) | data formatting | bytes 8388608 | tf_op jit(solution)/shard_map/reshape | solution.py:38
  24.3 6.7 %fusion.15 = f32[16,8,2,64,128]{4,3,0,2,1:T(8,128)} fusion(bf16[8,1,2,128,2,128]{5,0,4,3,2,1:T(8,128)(2,1)S(1)} %get-tuple-element.16, bf16[16,8,2,64,128]{4,3,2,1,0:T(8,128)(2,1)} %reshape.187), kind=kOutput, calls=%fused_computation.21 | convolution fusion | flops 1073741824 | bytes 13631488 | tf_op jit(solution)/shard_map/pcqbk,cqkon->pcobn/dot_general | solution.py:43
  31.0 4.7 slice.38
  35.7 0.0 copy-done.2
  35.7 2.9 fusion.2
  38.6 7.3 %convert_element_type.87 = bf16[16,8,2,8192]{3,0,2,1:T(8,128)(2,1)} reshape(bf16[16,8,2,64,128]{4,3,0,2,1:T(8,128)(2,1)} %fusion.2) | data formatting | bytes 8388608 | tf_op jit(solution)/shard_map/convert_element_type | solution.py:48
  45.9 4.1 constant_dynamic-slice_fusion
  50.0 2.5 collective-permute-start.6
  52.5 0.6 collective-permute-start.5
  53.1 0.0 collective-permute-start.2
  53.1 1.7 collective-permute-start.1
  54.8 0.2 collective-permute-start
  54.9 0.1 iota_add_fusion
  55.0 0.1 reshape.186
  55.1 0.2 reduce_window_sum.22
  55.3 0.1 convert_compare_fusion
  55.4 0.2 select_reduce_fusion
  55.6 0.0 copy-done.4
  55.6 0.1 copy.71
  55.7 0.0 copy-done
  55.7 1.4 convert_bitcast_fusion
  57.2 6.2 %broadcast_in_dim.13 = bf16[128,8,2,1024]{3,2,1,0:T(2,128)(2,1)} broadcast(bf16[]{:T(256)} %constant.31.clone.1), dimensions={} | broadcast | bytes 4194306 | tf_op jit(solution)/shard_map/broadcast_in_dim | solution.py:115
  63.4 1.3 copy_dynamic-update-slice_fusion.7
  64.7 0.1 copy.70
  64.8 0.1 maximum_maximum_fusion.1
  65.0 2.7 copy.46
  67.8 0.0 collective-permute-done
  67.8 2.4 collective-permute-start.3
  70.2 2.4 copy_dynamic-update-slice_fusion.6
  72.6 6.5 %collective-permute-done.1 = bf16[16,8,2,1024]{3,0,2,1:T(8,128)(2,1)} collective-permute-done((bf16[16,8,2,1024]{3,0,2,1:T(8,128)(2,1)}, bf16[16,8,2,1024]{3,0,2,1:T(8,128)(2,1)}, u32[]{:S(2)}, u32[]{:S(2)}) %collective-permute-start.1) | collective-permute-done | bytes 524320 | tf_op jit(solution)/shard_map/ppermute | solution.py:119
  79.1 1.5 collective-permute-start.4
  80.6 2.4 copy_dynamic-update-slice_fusion.5
  83.0 0.0 collective-permute-done.2
  83.0 2.4 copy_dynamic-update-slice_fusion.4
  85.4 7.2 %collective-permute-done.3 = bf16[16,8,2,1024]{3,0,2,1:T(8,128)(2,1)S(1)} collective-permute-done((bf16[16,8,2,1024]{3,0,2,1:T(8,128)(2,1)}, bf16[16,8,2,1024]{3,0,2,1:T(8,128)(2,1)S(1)}, u32[]{:S(2)}, u32[]{:S(2)}) %collective-permute-start.3) | collective-permute-done | bytes 524320 | tf_op jit(solution)/shard_map/ppermute | solution.py:119
  92.5 1.3 copy_dynamic-update-slice_fusion.3
  93.9 9.0 %collective-permute-done.4 = bf16[16,8,2,1024]{3,0,2,1:T(8,128)(2,1)S(1)} collective-permute-done((bf16[16,8,2,1024]{3,0,2,1:T(8,128)(2,1)S(1)}, bf16[16,8,2,1024]{3,0,2,1:T(8,128)(2,1)S(1)}, u32[]{:S(2)}, u32[]{:S(2)}) %collective-permute-start.4) | collective-permute-done | bytes 524320 | tf_op jit(solution)/shard_map/ppermute | solution.py:119
  102.8 1.3 copy_dynamic-update-slice_fusion.2
  104.2 0.0 collective-permute-done.5
  104.2 2.4 copy_dynamic-update-slice_fusion.1
  106.5 0.0 collective-permute-done.6
  106.5 2.4 copy_dynamic-update-slice_fusion
  108.9 7.4 %reshape.188 = bf16[16,128,1024]{2,1,0:T(8,128)(2,1)} reshape(bf16[128,8,2,1024]{3,2,1,0:T(2,128)(2,1)} %copy_dynamic-update-slice_fusion) | data formatting | bytes 8388608 | tf_op jit(solution)/shard_map/reshape | solution.py:54
  116.3 3.7 convolution_convert_fusion.3
  120.0 2.4 convolution_convert_fusion.2
  122.5 12.4 %convolution_convert_fusion.1 = bf16[4096,1024]{1,0:T(8,128)(2,1)} fusion(bf16[4096,1024]{1,0:T(8,128)(2,1)S(1)} %bitcast.130, bf16[128,8,8,128]{3,2,1,0:T(8,128)(2,1)} %bitcast.132), kind=kOutput, calls=%fused_computation.11 | convolution fusion | flops 8594128896 | bytes 18874368 | tf_op jit(solution)/shard_map/dot_general | solution.py:93
  134.9 8.2 %reshape_reshape.3 = bf16[16,262144]{1,0:T(8,128)(2,1)} reshape(bf16[4096,1024]{1,0:T(8,128)(2,1)} %convolution_convert_fusion.1) | data formatting | bytes 16777216 | tf_op jit(solution)/shard_map/reshape;reshape | solution.py:98
  143.1 13.6 %convolution_convert_fusion = bf16[32,262144]{1,0:T(8,128)(2,1)} fusion(pred[32,16]{1,0:T(32,128)(4,1)S(1)} %and.50, bf16[16,262144]{1,0:T(8,128)(2,1)} %reshape_reshape.3), kind=kOutput, calls=%fused_computation | convolution fusion | flops 276824064 | bytes 25166336 | tf_op jit(solution)/shard_map/dot_general | solution.py:98
  156.7 18.7 %copy.73 = bf16[4,8,256,1024]{3,2,1,0:T(8,128)(2,1)} copy(bf16[4,8,256,1024]{3,1,2,0:T(8,128)(2,1)} %bitcast.128) | data formatting | bytes 33554432
  175.4 7.9 %all-to-all-start = ((bf16[32,2,128,1024]{3,2,1,0:T(8,128)(2,1)}), bf16[32,2,128,1024]{3,2,1,0:T(8,128)(2,1)}, u32[]{:S(2)}, u32[]{:S(2)}) async-start(bf16[32,2,128,1024]{3,2,1,0:T(8,128)(2,1)} %bitcast.127), calls=%async_computation | async-start | bytes 33554432 | tf_op jit(solution)/shard_map/all_to_all | solution.py:150
  183.3 0.1 eq.166
  183.4 0.2 convolution_convert_fusion.4
  183.6 300.3 %all-to-all-done = bf16[32,2,128,1024]{3,2,1,0:T(8,128)(2,1)} async-done(((bf16[32,2,128,1024]{3,2,1,0:T(8,128)(2,1)}), bf16[32,2,128,1024]{3,2,1,0:T(8,128)(2,1)}, u32[]{:S(2)}, u32[]{:S(2)}) %all-to-all-start) | async-done | bytes 16777248 | tf_op jit(solution)/shard_map/all_to_all | solution.py:150
  483.9 16.6 %fusion.20 = bf16[8,2,128,1024]{3,0,2,1:T(8,128)(2,1)S(1)} fusion(bf16[8,32,1,1]{0,1,3,2:T(8,128)(2,1)S(1)} %bitcast.137, bf16[2,128,1024,32]{2,1,0,3:T(8,128)(2,1)} %bitcast.75), kind=kOutput, calls=%fused_computation.22 | convolution fusion | flops 136314880 | bytes 20972032 | tf_op jit(solution)/shard_map/dot_general | solution.py:151
  500.5 4.4 copy.49
  504.9 0.0 copy-done.1
  (28 shorter events, 0.2 us)
Async XLA Ops:
  0.0 55.7 %copy-start = (bf16[8,384,128]{2,1,0:T(8,128)(2,1)S(1)}, bf16[8,384,128]{2,1,0:T(8,128)(2,1)}, u32[]{:S(2)}) copy-start(bf16[8,384,128]{2,1,0:T(8,128)(2,1)} %param.12) | copy-start | bytes 2359300
  31.0 4.7 copy-start.2
  45.9 9.0 %copy-start.8 = (s32[8]{0:T(128)S(1)}, s32[8]{0:T(128)}, u32[]{:S(2)}) copy-start(s32[8]{0:T(128)} %param.13) | copy-start | bytes 100
  45.9 9.1 %copy-start.6 = (s32[256]{0:T(256)S(1)}, s32[256]{0:T(256)}, u32[]{:S(2)}) copy-start(s32[256]{0:T(256)} %param.14) | copy-start | bytes 3076
  45.9 9.7 %copy-start.4 = (bf16[2,64,64]{2,1,0:T(8,128)(2,1)S(1)}, bf16[2,64,64]{2,1,0:T(8,128)(2,1)}, u32[]{:S(2)}) copy-start(bf16[2,64,64]{2,1,0:T(8,128)(2,1)} %param.10) | copy-start | bytes 49156
  45.9 9.8 %copy-start.5 = (bf16[2,128,64]{1,2,0:T(8,128)(2,1)S(1)}, bf16[2,128,64]{1,2,0:T(8,128)(2,1)}, u32[]{:S(2)}) copy-start(bf16[2,128,64]{1,2,0:T(8,128)(2,1)} %param.11) | copy-start | bytes 98308
  50.0 56.5 %collective-permute-start.6 = (bf16[16,8,2,1024]{3,0,2,1:T(8,128)(2,1)}, bf16[16,8,2,1024]{3,0,2,1:T(8,128)(2,1)}, u32[]{:S(2)}, u32[]{:S(2)}) collective-permute-start(bf16[16,8,2,1024]{3,0,2,1:T(8,128)(2,1)} %get-tuple-element.7), channel_id=1, source_target_pairs={{0,7},{1,6},{2,5},{3,4},{4,3},{5,2},{6,1},{7,0},{8,15},{9,14},{10,... | collective-permute-start | bytes 1572872 | tf_op jit(solution)/shard_map/ppermute | solution.py:119
  52.5 51.7 %collective-permute-start.5 = (bf16[16,8,2,1024]{3,0,2,1:T(8,128)(2,1)}, bf16[16,8,2,1024]{3,0,2,1:T(8,128)(2,1)}, u32[]{:S(2)}, u32[]{:S(2)}) collective-permute-start(bf16[16,8,2,1024]{3,0,2,1:T(8,128)(2,1)} %get-tuple-element.8), channel_id=1, source_target_pairs={{0,6},{1,7},{2,4},{3,5},{4,2},{5,3},{6,0},{7,1},{8,14},{9,15},{10,... | collective-permute-start | bytes 1572872 | tf_op jit(solution)/shard_map/ppermute | solution.py:119
  53.1 29.9 %collective-permute-start.2 = (bf16[16,8,2,1024]{3,0,2,1:T(8,128)(2,1)}, bf16[16,8,2,1024]{3,0,2,1:T(8,128)(2,1)}, u32[]{:S(2)}, u32[]{:S(2)}) collective-permute-start(bf16[16,8,2,1024]{3,0,2,1:T(8,128)(2,1)} %get-tuple-element.11), channel_id=1, source_target_pairs={{0,3},{1,2},{2,1},{3,0},{4,7},{5,6},{6,5},{7,4},{8,11},{9,10},{10,... | collective-permute-start | bytes 1572872 | tf_op jit(solution)/shard_map/ppermute | solution.py:119
  53.1 26.0 %collective-permute-start.1 = (bf16[16,8,2,1024]{3,0,2,1:T(8,128)(2,1)}, bf16[16,8,2,1024]{3,0,2,1:T(8,128)(2,1)}, u32[]{:S(2)}, u32[]{:S(2)}) collective-permute-start(bf16[16,8,2,1024]{3,0,2,1:T(8,128)(2,1)} %get-tuple-element.12), channel_id=1, source_target_pairs={{0,2},{1,3},{2,0},{3,1},{4,6},{5,7},{6,4},{7,5},{8,10},{9,11},{10,... | collective-permute-start | bytes 1572872 | tf_op jit(solution)/shard_map/ppermute | solution.py:119
  54.8 13.0 %collective-permute-start = (bf16[16,8,2,1024]{3,0,2,1:T(8,128)(2,1)}, bf16[16,8,2,1024]{3,0,2,1:T(8,128)(2,1)}, u32[]{:S(2)}, u32[]{:S(2)}) collective-permute-start(bf16[16,8,2,1024]{3,0,2,1:T(8,128)(2,1)} %get-tuple-element.13), channel_id=1, source_target_pairs={{0,1},{1,0},{2,3},{3,2},{4,5},{5,4},{6,7},{7,6},{8,9},{9,8},{10,11... | collective-permute-start | bytes 1572872 | tf_op jit(solution)/shard_map/ppermute | solution.py:119
  64.7 14.4 %copy-start.3 = (bf16[16,8,2,1024]{3,0,2,1:T(8,128)(2,1)S(1)}, bf16[16,8,2,1024]{3,0,2,1:T(8,128)(2,1)}, u32[]{:S(2)}) copy-start(bf16[16,8,2,1024]{3,0,2,1:T(8,128)(2,1)} %get-tuple-element.9) | copy-start | bytes 1572868
  67.8 24.8 %collective-permute-start.3 = (bf16[16,8,2,1024]{3,0,2,1:T(8,128)(2,1)}, bf16[16,8,2,1024]{3,0,2,1:T(8,128)(2,1)S(1)}, u32[]{:S(2)}, u32[]{:S(2)}) collective-permute-start(bf16[16,8,2,1024]{3,0,2,1:T(8,128)(2,1)} %get-tuple-element.10), channel_id=1, source_target_pairs={{0,4},{1,5},{2,6},{3,7},{4,0},{5,1},{6,2},{7,3},{8,12},{9,13},{10,... | collective-permute-start | bytes 1572872 | tf_op jit(solution)/shard_map/ppermute | solution.py:119
  79.1 23.7 %collective-permute-start.4 = (bf16[16,8,2,1024]{3,0,2,1:T(8,128)(2,1)S(1)}, bf16[16,8,2,1024]{3,0,2,1:T(8,128)(2,1)S(1)}, u32[]{:S(2)}, u32[]{:S(2)}) collective-permute-start(bf16[16,8,2,1024]{3,0,2,1:T(8,128)(2,1)S(1)} %copy-done.3), channel_id=1, source_target_pairs={{0,5},{1,4},{2,7},{3,6},{4,1},{5,0},{6,3},{7,2},{8,13},{9,12},{10,... | collective-permute-start | bytes 1572872 | tf_op jit(solution)/shard_map/ppermute | solution.py:119
  175.4 7.9 %copy-start.7 = (s32[256]{0:T(256)S(1)}, s32[256]{0:T(256)}, u32[]{:S(2)}) copy-start(s32[256]{0:T(256)} %param.15) | copy-start | bytes 3076
  175.4 308.5 %all-to-all-start = ((bf16[32,2,128,1024]{3,2,1,0:T(8,128)(2,1)}), bf16[32,2,128,1024]{3,2,1,0:T(8,128)(2,1)}, u32[]{:S(2)}, u32[]{:S(2)}) async-start(bf16[32,2,128,1024]{3,2,1,0:T(8,128)(2,1)} %bitcast.127), calls=%async_computation | async-start | bytes 33554432 | tf_op jit(solution)/shard_map/all_to_all | solution.py:150
  483.9 21.0 %copy-start.1 = (bf16[8,384,128]{2,1,0:T(8,128)(2,1)S(1)}, bf16[8,384,128]{2,1,0:T(8,128)(2,1)}, u32[]{:S(2)}) copy-start(bf16[8,384,128]{2,1,0:T(8,128)(2,1)} %param.12) | copy-start | bytes 2359300
